TPU v7x, 32 devices: a whole 2x2x4 slice. The times are simulated.
32 devices in a mesh: site: 4 (over y, x), bond: 8 (over z, core).
Axes of the slice: x: 2, y: 2, z: 4, core: 2. Of those that a mesh axis runs over, the one named last changes fastest.
Arguments:
- start_rows: bfloat16 [1024, 4096], P(None, 'bond'), may hold values from -6 to 6
- site_tensors: bfloat16 [4, 4096, 8, 4096], P('site', None, None, 'bond'), may hold values from -0.09375 to 0.09375
- block_scales: float32 [4, 8, 32], P('site', None, 'bond'), may hold values from 0.25 to 1
- displacement: float32 [4, 8, 8], P('site'), may hold values from -0.9 to 0.9
- outcomes: int32 [4, 1024], P('site'), may hold values from 0 to 7
Outputs:
- leaving: bfloat16 [4, 1024, 4096], P('site', None, 'bond')
- log_norms: float32 [4, 1024], P('site')
Inputs may be any that keep to these rules, and one draw needn't show every extreme that they name: outcomes index the second dimension of displacement.
All inputs are finite; a program needn't handle non-finite values.
Results may differ from a plain program's by a relative error of at most 0.014.
Values may be sent and summed in bfloat16 or wider, within the bound.
A program may use at most 128 MiB of HBM per device.

v0:
```python
import jax
import jax.numpy as jnp
from jax import lax
from jax.sharding import PartitionSpec as P

ROWS = 512


def shifted(value, axis, steps):
    count = lax.axis_size(axis)
    initial, last = (max(0, -steps), min(count, count - steps))
    return lax.ppermute(value, axis, [(source, source + steps) for source in range(initial, last)])


def local(start_rows, site_tensors, block_scales, displacement, outcomes):
    sites = lax.axis_size("site")
    cols = site_tensors.shape[3]
    chi = site_tensors.shape[1]
    phys = site_tensors.shape[2]
    nblk = block_scales.shape[2]
    allrows = start_rows.shape[0]
    grows = ROWS
    ngroups = allrows // grows
    ticks = ngroups + sites - 1
    a_mat = site_tensors[0].reshape(chi, phys * cols)
    scales = block_scales[0][:, :, None]
    table = displacement[0]
    outcome_row = outcomes[0]
    position = lax.axis_index("site")

    def tick(step, carry):
        incoming, incoming_norm, out_leave, out_logs = carry
        batch = step - position
        valid = jnp.logical_and(batch >= 0, batch < ngroups)
        first = jnp.clip(batch, 0, ngroups - 1) * grows
        start_piece = lax.dynamic_slice_in_dim(start_rows, first, grows, 0)
        rows_in = jnp.where(position == 0, start_piece, incoming)
        piece = lax.all_gather(rows_in, "bond", axis=1, tiled=True)
        total = jnp.dot(piece, a_mat, preferred_element_type=jnp.float32)
        pf = piece.astype(jnp.float32)
        total, squares = (total, jnp.sum(pf * pf, axis=1))
        local_norm = jnp.sqrt(squares / chi + 1e-06)
        prod = total.reshape(grows, phys, nblk, cols // nblk) * scales[None]
        prod = prod.reshape(grows, phys, cols)
        picked = lax.dynamic_slice_in_dim(outcome_row, first, grows, 0)
        onehot = (picked[:, None] == jnp.arange(phys, dtype=jnp.int32)[None, :]).astype(jnp.float32)
        weight = jnp.dot(onehot, table, precision=lax.Precision.HIGHEST)
        mixed = jnp.sum(weight[:, :, None] * prod, axis=1)
        leave = (mixed / local_norm[:, None]).astype(jnp.bfloat16)
        out_leave = jnp.where(
            valid, lax.dynamic_update_slice_in_dim(out_leave, leave, first, 0), out_leave
        )
        out_logs = jnp.where(
            valid,
            lax.dynamic_update_slice_in_dim(out_logs, jnp.log(local_norm), first, 0),
            out_logs,
        )
        incoming = shifted(leave, "site", 1)
        return (incoming, incoming_norm, out_leave, out_logs)

    carry = (
        jnp.zeros((grows, cols), jnp.bfloat16),
        jnp.ones((grows,), jnp.float32),
        jnp.zeros((allrows, cols), jnp.bfloat16),
        jnp.zeros((allrows,), jnp.float32),
    )
    carry = lax.fori_loop(0, ticks, tick, carry)
    return (carry[2][None], carry[3][None])


def solution(mesh):
    return jax.shard_map(
        local,
        mesh=mesh,
        in_specs=(
            P(None, "bond"),
            P("site", None, None, "bond"),
            P("site", None, "bond"),
            P("site", None, None),
            P("site", None),
        ),
        out_specs=(P("site", None, "bond"), P("site", None)),
        check_vma=False,
    )
```

profile of v0, /device:TPU:7, one launch (start us, length us, event | category | flops | bytes accessed | tf_op | source)
XLA Modules:
  0.0 549.1 jit_solution(6089565585654436752)
XLA Ops:
  7.2 22.7 %copy.10 = bf16[512,8,8,512]{3,1,2,0:T(8,128)(2,1)} copy(bf16[512,8,8,512]{3,2,1,0:T(8,128)(2,1)} %bitcast.35) | data formatting | bytes 67108864
  31.1 510.9 %while.18 = (s32[]{:T(128)}, bf16[512,512]{1,0:T(8,128)(2,1)S(1)}, bf16[1024,512]{1,0:T(8,128)(2,1)}, f32[1024]{0:T(1024)S(1)}, s32[]{:T(128)}, /*index=5*/s32[1...) while((s32[]{:T(128)}, bf16[512,512]{1,0:T(8,128)(2,1)S(1)}, ...), condition=%wide.region_3.4_spmd, body=%wide.region_0.3_spmd.sunk | while | flops 17193637888 | bytes 113855224 | solution.py:67
  33.6 48.3 %all-gather.2.cloned.1.call-done = bf16[512,4096]{1,0:T(8,128)(2,1)} async-done(((bf16[512,512]{1,0:T(8,128)(2,1)}), bf16[512,4096]{1,0:T(8,128)(2,1)}) %all-gather.2.cloned.1.call-update) | async-done | bytes 4194320 | tf_op jit(solution)/shard_map/while/body/eval_jaxpr/all_gather | solution.py:38
  82.0 22.6 %fusion.18 = f32[512,4096]{1,0:T(8,128)S(1)} fusion(bf16[512,4096]{1,0:T(8,128)(2,1)} %all-gather.2.cloned.1.call-done, bf16[4096,4096]{1,0:T(8,128)(2,1)} %get-tuple-element.361), kind=kOutput, calls=%fused_computation.14.clone.1 | convolution fusion | flops 17179869184 | bytes 46137344 | tf_op jit(solution)/shard_map/while/body/eval_jaxpr/dot_general | solution.py:39
  104.6 8.2 %copy.12 = f32[64,8,8,512]{3,2,1,0:T(8,128)S(1)} copy(f32[64,8,8,512]{3,1,2,0:T(8,128)S(1)} %bitcast.34) | data formatting | bytes 16777216 | tf_op jit(solution)/shard_map/while
  113.8 3.9 fusion.20
  121.1 13.8 %collective-permute-done = bf16[512,512]{1,0:T(8,128)(2,1)S(1)} collective-permute-done((bf16[512,512]{1,0:T(8,128)(2,1)S(1)}, bf16[512,512]{1,0:T(8,128)(2,1)S(1)}, u32[]{:S(2)}, u32[]{:S(2)}) %collective-permute-start) | collective-permute-done | bytes 524320 | tf_op jit(solution)/shard_map/while/body/eval_jaxpr/ppermute | solution.py:12
  137.4 46.5 %all-gather.2.cloned.1.call-done = bf16[512,4096]{1,0:T(8,128)(2,1)} async-done(((bf16[512,512]{1,0:T(8,128)(2,1)}), bf16[512,4096]{1,0:T(8,128)(2,1)}) %all-gather.2.cloned.1.call-update) | async-done | bytes 4194320 | tf_op jit(solution)/shard_map/while/body/eval_jaxpr/all_gather | solution.py:38
  183.9 22.6 %fusion.18 = f32[512,4096]{1,0:T(8,128)S(1)} fusion(bf16[512,4096]{1,0:T(8,128)(2,1)} %all-gather.2.cloned.1.call-done, bf16[4096,4096]{1,0:T(8,128)(2,1)} %get-tuple-element.361), kind=kOutput, calls=%fused_computation.14.clone.1 | convolution fusion | flops 17179869184 | bytes 46137344 | tf_op jit(solution)/shard_map/while/body/eval_jaxpr/dot_general | solution.py:39
  206.5 8.2 %copy.12 = f32[64,8,8,512]{3,2,1,0:T(8,128)S(1)} copy(f32[64,8,8,512]{3,1,2,0:T(8,128)S(1)} %bitcast.34) | data formatting | bytes 16777216 | tf_op jit(solution)/shard_map/while
  223.0 13.8 %collective-permute-done = bf16[512,512]{1,0:T(8,128)(2,1)S(1)} collective-permute-done((bf16[512,512]{1,0:T(8,128)(2,1)S(1)}, bf16[512,512]{1,0:T(8,128)(2,1)S(1)}, u32[]{:S(2)}, u32[]{:S(2)}) %collective-permute-start) | collective-permute-done | bytes 524320 | tf_op jit(solution)/shard_map/while/body/eval_jaxpr/ppermute | solution.py:12
  239.3 46.5 %all-gather.2.cloned.1.call-done = bf16[512,4096]{1,0:T(8,128)(2,1)} async-done(((bf16[512,512]{1,0:T(8,128)(2,1)}), bf16[512,4096]{1,0:T(8,128)(2,1)}) %all-gather.2.cloned.1.call-update) | async-done | bytes 4194320 | tf_op jit(solution)/shard_map/while/body/eval_jaxpr/all_gather | solution.py:38
  285.8 22.6 %fusion.18 = f32[512,4096]{1,0:T(8,128)S(1)} fusion(bf16[512,4096]{1,0:T(8,128)(2,1)} %all-gather.2.cloned.1.call-done, bf16[4096,4096]{1,0:T(8,128)(2,1)} %get-tuple-element.361), kind=kOutput, calls=%fused_computation.14.clone.1 | convolution fusion | flops 17179869184 | bytes 46137344 | tf_op jit(solution)/shard_map/while/body/eval_jaxpr/dot_general | solution.py:39
  308.4 8.2 %copy.12 = f32[64,8,8,512]{3,2,1,0:T(8,128)S(1)} copy(f32[64,8,8,512]{3,1,2,0:T(8,128)S(1)} %bitcast.34) | data formatting | bytes 16777216 | tf_op jit(solution)/shard_map/while
  324.9 13.8 %collective-permute-done = bf16[512,512]{1,0:T(8,128)(2,1)S(1)} collective-permute-done((bf16[512,512]{1,0:T(8,128)(2,1)S(1)}, bf16[512,512]{1,0:T(8,128)(2,1)S(1)}, u32[]{:S(2)}, u32[]{:S(2)}) %collective-permute-start) | collective-permute-done | bytes 524320 | tf_op jit(solution)/shard_map/while/body/eval_jaxpr/ppermute | solution.py:12
  341.2 46.2 %all-gather.2.cloned.1.call-done = bf16[512,4096]{1,0:T(8,128)(2,1)} async-done(((bf16[512,512]{1,0:T(8,128)(2,1)}), bf16[512,4096]{1,0:T(8,128)(2,1)}) %all-gather.2.cloned.1.call-update) | async-done | bytes 4194320 | tf_op jit(solution)/shard_map/while/body/eval_jaxpr/all_gather | solution.py:38
  387.4 22.6 %fusion.18 = f32[512,4096]{1,0:T(8,128)S(1)} fusion(bf16[512,4096]{1,0:T(8,128)(2,1)} %all-gather.2.cloned.1.call-done, bf16[4096,4096]{1,0:T(8,128)(2,1)} %get-tuple-element.361), kind=kOutput, calls=%fused_computation.14.clone.1 | convolution fusion | flops 17179869184 | bytes 46137344 | tf_op jit(solution)/shard_map/while/body/eval_jaxpr/dot_general | solution.py:39
  410.0 8.2 %copy.12 = f32[64,8,8,512]{3,2,1,0:T(8,128)S(1)} copy(f32[64,8,8,512]{3,1,2,0:T(8,128)S(1)} %bitcast.34) | data formatting | bytes 16777216 | tf_op jit(solution)/shard_map/while
  426.6 13.8 %collective-permute-done = bf16[512,512]{1,0:T(8,128)(2,1)S(1)} collective-permute-done((bf16[512,512]{1,0:T(8,128)(2,1)S(1)}, bf16[512,512]{1,0:T(8,128)(2,1)S(1)}, u32[]{:S(2)}, u32[]{:S(2)}) %collective-permute-start) | collective-permute-done | bytes 524320 | tf_op jit(solution)/shard_map/while/body/eval_jaxpr/ppermute | solution.py:12
  442.9 46.2 %all-gather.2.cloned.1.call-done = bf16[512,4096]{1,0:T(8,128)(2,1)} async-done(((bf16[512,512]{1,0:T(8,128)(2,1)}), bf16[512,4096]{1,0:T(8,128)(2,1)}) %all-gather.2.cloned.1.call-update) | async-done | bytes 4194320 | tf_op jit(solution)/shard_map/while/body/eval_jaxpr/all_gather | solution.py:38
  489.1 22.6 %fusion.18 = f32[512,4096]{1,0:T(8,128)S(1)} fusion(bf16[512,4096]{1,0:T(8,128)(2,1)} %all-gather.2.cloned.1.call-done, bf16[4096,4096]{1,0:T(8,128)(2,1)} %get-tuple-element.361), kind=kOutput, calls=%fused_computation.14.clone.1 | convolution fusion | flops 17179869184 | bytes 46137344 | tf_op jit(solution)/shard_map/while/body/eval_jaxpr/dot_general | solution.py:39
  511.7 8.2 %copy.12 = f32[64,8,8,512]{3,2,1,0:T(8,128)S(1)} copy(f32[64,8,8,512]{3,1,2,0:T(8,128)S(1)} %bitcast.34) | data formatting | bytes 16777216 | tf_op jit(solution)/shard_map/while
  520.9 3.9 fusion.20
  528.2 13.8 %collective-permute-done = bf16[512,512]{1,0:T(8,128)(2,1)S(1)} collective-permute-done((bf16[512,512]{1,0:T(8,128)(2,1)S(1)}, bf16[512,512]{1,0:T(8,128)(2,1)S(1)}, u32[]{:S(2)}, u32[]{:S(2)}) %collective-permute-start) | collective-permute-done | bytes 524320 | tf_op jit(solution)/shard_map/while/body/eval_jaxpr/ppermute | solution.py:12
  (74 shorter events, 48.0 us)
Async XLA Ops:
  7.2 23.9 %copy-start.1 = (f32[1,8,8]{2,1,0:T(8,128)S(1)}, f32[1,8,8]{2,1,0:T(8,128)}, u32[]{:S(2)}) copy-start(f32[1,8,8]{2,1,0:T(8,128)} %param.10) | copy-start | bytes 772
  7.2 23.9 %copy-start.2 = (f32[1,8,4]{1,2,0:T(4,128)S(1)}, f32[1,8,4]{1,2,0:T(4,128)}, u32[]{:S(2)}) copy-start(f32[1,8,4]{1,2,0:T(4,128)} %param.9) | copy-start | bytes 388
  7.2 23.9 %copy-start.4 = (s32[1,1024]{1,0:T(1,128)S(1)}, s32[1,1024]{1,0:T(1,128)}, u32[]{:S(2)}) copy-start(s32[1,1024]{1,0:T(1,128)} %param.11) | copy-start | bytes 12292
  31.1 50.9 %all-gather.2.cloned.1.call-start = ((), (), s32[]{:S(2)}) async-start(), calls=%async_computation | async-start | bytes 4718592 | tf_op jit(solution)/shard_map/while/body/eval_jaxpr/all_gather | solution.py:38
  104.6 8.2 %copy-start = (bf16[512,4096]{1,0:T(8,128)(2,1)S(1)}, bf16[512,4096]{1,0:T(8,128)(2,1)}, u32[]{:S(2)}) copy-start(bf16[512,4096]{1,0:T(8,128)(2,1)} %all-gather.2.cloned.1.call-done) | copy-start | bytes 12582916 | tf_op jit(solution)/shard_map/while
  119.8 15.1 %collective-permute-start = (bf16[512,512]{1,0:T(8,128)(2,1)S(1)}, bf16[512,512]{1,0:T(8,128)(2,1)S(1)}, u32[]{:S(2)}, u32[]{:S(2)}) collective-permute-start(bf16[512,512]{1,0:T(8,128)(2,1)S(1)} %get-tuple-element.317), channel_id=1, source_target_pairs={{0,8},{8,16},{16,24},{1,9},{9,17},{17,25},{2,10},{10,18},{18,26},{... | collective-permute-start | bytes 1572872 | tf_op jit(solution)/shard_map/while/body/eval_jaxpr/ppermute | solution.py:12
  134.9 49.0 %all-gather.2.cloned.1.call-start = ((), (), s32[]{:S(2)}) async-start(), calls=%async_computation | async-start | bytes 4718592 | tf_op jit(solution)/shard_map/while/body/eval_jaxpr/all_gather | solution.py:38
  206.5 8.2 %copy-start = (bf16[512,4096]{1,0:T(8,128)(2,1)S(1)}, bf16[512,4096]{1,0:T(8,128)(2,1)}, u32[]{:S(2)}) copy-start(bf16[512,4096]{1,0:T(8,128)(2,1)} %all-gather.2.cloned.1.call-done) | copy-start | bytes 12582916 | tf_op jit(solution)/shard_map/while
  221.7 15.1 %collective-permute-start = (bf16[512,512]{1,0:T(8,128)(2,1)S(1)}, bf16[512,512]{1,0:T(8,128)(2,1)S(1)}, u32[]{:S(2)}, u32[]{:S(2)}) collective-permute-start(bf16[512,512]{1,0:T(8,128)(2,1)S(1)} %get-tuple-element.317), channel_id=1, source_target_pairs={{0,8},{8,16},{16,24},{1,9},{9,17},{17,25},{2,10},{10,18},{18,26},{... | collective-permute-start | bytes 1572872 | tf_op jit(solution)/shard_map/while/body/eval_jaxpr/ppermute | solution.py:12
  236.8 49.0 %all-gather.2.cloned.1.call-start = ((), (), s32[]{:S(2)}) async-start(), calls=%async_computation | async-start | bytes 4718592 | tf_op jit(solution)/shard_map/while/body/eval_jaxpr/all_gather | solution.py:38
  308.4 8.2 %copy-start = (bf16[512,4096]{1,0:T(8,128)(2,1)S(1)}, bf16[512,4096]{1,0:T(8,128)(2,1)}, u32[]{:S(2)}) copy-start(bf16[512,4096]{1,0:T(8,128)(2,1)} %all-gather.2.cloned.1.call-done) | copy-start | bytes 12582916 | tf_op jit(solution)/shard_map/while
  323.6 15.1 %collective-permute-start = (bf16[512,512]{1,0:T(8,128)(2,1)S(1)}, bf16[512,512]{1,0:T(8,128)(2,1)S(1)}, u32[]{:S(2)}, u32[]{:S(2)}) collective-permute-start(bf16[512,512]{1,0:T(8,128)(2,1)S(1)} %get-tuple-element.317), channel_id=1, source_target_pairs={{0,8},{8,16},{16,24},{1,9},{9,17},{17,25},{2,10},{10,18},{18,26},{... | collective-permute-start | bytes 1572872 | tf_op jit(solution)/shard_map/while/body/eval_jaxpr/ppermute | solution.py:12
  338.7 48.7 %all-gather.2.cloned.1.call-start = ((), (), s32[]{:S(2)}) async-start(), calls=%async_computation | async-start | bytes 4718592 | tf_op jit(solution)/shard_map/while/body/eval_jaxpr/all_gather | solution.py:38
  410.0 8.2 %copy-start = (bf16[512,4096]{1,0:T(8,128)(2,1)S(1)}, bf16[512,4096]{1,0:T(8,128)(2,1)}, u32[]{:S(2)}) copy-start(bf16[512,4096]{1,0:T(8,128)(2,1)} %all-gather.2.cloned.1.call-done) | copy-start | bytes 12582916 | tf_op jit(solution)/shard_map/while
  425.3 15.1 %collective-permute-start = (bf16[512,512]{1,0:T(8,128)(2,1)S(1)}, bf16[512,512]{1,0:T(8,128)(2,1)S(1)}, u32[]{:S(2)}, u32[]{:S(2)}) collective-permute-start(bf16[512,512]{1,0:T(8,128)(2,1)S(1)} %get-tuple-element.317), channel_id=1, source_target_pairs={{0,8},{8,16},{16,24},{1,9},{9,17},{17,25},{2,10},{10,18},{18,26},{... | collective-permute-start | bytes 1572872 | tf_op jit(solution)/shard_map/while/body/eval_jaxpr/ppermute | solution.py:12
  440.4 48.7 %all-gather.2.cloned.1.call-start = ((), (), s32[]{:S(2)}) async-start(), calls=%async_computation | async-start | bytes 4718592 | tf_op jit(solution)/shard_map/while/body/eval_jaxpr/all_gather | solution.py:38
  511.7 8.2 %copy-start = (bf16[512,4096]{1,0:T(8,128)(2,1)S(1)}, bf16[512,4096]{1,0:T(8,128)(2,1)}, u32[]{:S(2)}) copy-start(bf16[512,4096]{1,0:T(8,128)(2,1)} %all-gather.2.cloned.1.call-done) | copy-start | bytes 12582916 | tf_op jit(solution)/shard_map/while
  526.9 15.1 %collective-permute-start = (bf16[512,512]{1,0:T(8,128)(2,1)S(1)}, bf16[512,512]{1,0:T(8,128)(2,1)S(1)}, u32[]{:S(2)}, u32[]{:S(2)}) collective-permute-start(bf16[512,512]{1,0:T(8,128)(2,1)S(1)} %get-tuple-element.317), channel_id=1, source_target_pairs={{0,8},{8,16},{16,24},{1,9},{9,17},{17,25},{2,10},{10,18},{18,26},{... | collective-permute-start | bytes 1572872 | tf_op jit(solution)/shard_map/while/body/eval_jaxpr/ppermute | solution.py:12
  542.0 0.6 copy-start.3
Sparse Core Ops, SparseCore 0:
  33.5 48.4 all-gather.1
  137.3 46.5 all-gather.1
  239.2 46.5 all-gather.1
  340.9 46.5 all-gather.1
  442.5 46.5 all-gather.1
where the time goes:
time: 551 us; the launch traced here: 549 us
  waiting for transfers between devices  303 us (55%)
  matrix products  115 us (21%)
  local copies, waits for them, and re-layouts  66 us (12%)
  other arithmetic  45.2 us (8%)
  between operations  13.8 us (3%)
  starting transfers between devices  6.45 us (1%)
    all_gather x5, waiting for transfers between devices, tick(): piece = lax.all_gather(rows_in, 'bond', axis=1, tiled=True)  234 us
    dot_general x5, matrix products, tick(): total = jnp.dot(piece, a_mat, preferred_element_type=jnp.float32)  113 us
    ppermute x5, waiting for transfers between devices, shifted(): lax.ppermute(value, axis, [(source, source + steps) for source in range(i...  69 us
    while x15, local copies, waits for them, and re-layouts  40.9 us
    unnamed x9, local copies, waits for them, and re-layouts  23.3 us
    reduce_sum x5, other arithmetic, tick(): mixed = jnp.sum(weight[:, :, None] * prod, axis=1)  19.5 us
  transfers between devices with their start and end apart: 10, of which 10 were waited for; matrix products, arithmetic and copies ran while one was open for 0% of the time, Pallas kernels for 0%

commit v1 on v0

v1 whole, which is shorter than its diff:
```python
import functools
import jax
import jax.numpy as jnp
from jax import lax
from jax.experimental import pallas as pl
from jax.experimental.pallas import tpu as pltpu
from jax.sharding import PartitionSpec as P

ROWS = 128
CHUNK = 64
SLOTS = 4
LANES = 128
MESH = pl.DeviceIdType.MESH


def kernel(sites, bond, start_hbm, tensor_hbm, scale_ref, weight_ref, leave_ref, log_ref,
           mats, gathered, landing, wide, total,
           start_sem, load_sem, send_up, send_down, send_pair, send_site,
           recv_line, recv_pair, recv_site):
    chi, phys, cols = tensor_hbm.shape
    allrows = leave_ref.shape[0]
    rows = min(ROWS, allrows)
    batches = allrows // rows
    chips = bond // 2
    site = lax.axis_index("site")
    me = lax.axis_index("bond")
    chip = me // 2
    core = me % 2
    pair = me + 1 - 2 * core
    has_up = chip < chips - 1
    has_down = chip > 0
    first_site = site == 0
    has_next = site < sites - 1

    def block(ref, b, owner):
        return ref.at[pl.ds(pl.multiple_of(b * rows, rows), rows),
                      pl.ds(pl.multiple_of(owner * cols, cols), cols)]

    def up_copy(b, source):
        piece = block(gathered, b, 2 * source + core)
        return pltpu.make_async_remote_copy(
            piece, piece, send_up.at[b, source], recv_line.at[b, source],
            device_id={"bond": me + 2}, device_id_type=MESH)

    def down_copy(b, source):
        piece = block(gathered, b, 2 * source + core)
        return pltpu.make_async_remote_copy(
            piece, piece, send_down.at[b, source], recv_line.at[b, source],
            device_id={"bond": me - 2}, device_id_type=MESH)

    def pair_copy(b, source):
        piece = block(gathered, b, 2 * source + core)
        return pltpu.make_async_remote_copy(
            piece, piece, send_pair.at[b, source], recv_pair.at[b, source],
            device_id={"bond": pair}, device_id_type=MESH)

    def site_copy(b):
        return pltpu.make_async_remote_copy(
            leave_ref.at[pl.ds(pl.multiple_of(b * rows, rows), rows), :],
            block(gathered, b, me), send_site.at[b], recv_site.at[b],
            device_id={"site": site + 1}, device_id_type=MESH)

    def arrived_line(b, source):
        piece = block(gathered, b, 2 * source + core)
        pltpu.make_async_remote_copy(
            piece, piece, send_up.at[b, source], recv_line.at[b, source],
            device_id={"bond": pair}, device_id_type=MESH).wait_recv()

    def arrived_pair(b, source):
        piece = block(gathered, b, 2 * source + 1 - core)
        pltpu.make_async_remote_copy(
            piece, piece, send_pair.at[b, source], recv_pair.at[b, source],
            device_id={"bond": pair}, device_id_type=MESH).wait_recv()

    def relay(b, hop):
        if hop == 0:
            @pl.when(jnp.logical_not(first_site))
            def _():
                piece = block(gathered, b, me)
                pltpu.make_async_remote_copy(
                    piece, piece, send_site.at[b], recv_site.at[b],
                    device_id={"bond": pair}, device_id_type=MESH).wait_recv()

            @pl.when(has_up)
            def _():
                up_copy(b, chip).start()

            @pl.when(has_down)
            def _():
                down_copy(b, chip).start()

            pair_copy(b, chip).start()
            return

        @pl.when(chip - hop >= 0)
        def _():
            arrived_line(b, chip - hop)

            @pl.when(has_up)
            def _():
                up_copy(b, chip - hop).start()

            pair_copy(b, chip - hop).start()

        @pl.when(chip + hop < chips)
        def _():
            arrived_line(b, chip + hop)

            @pl.when(has_down)
            def _():
                down_copy(b, chip + hop).start()

            pair_copy(b, chip + hop).start()

    def load(step, slot):
        return pltpu.make_async_copy(
            tensor_hbm.at[pl.ds(pl.multiple_of(step * CHUNK, CHUNK), CHUNK)],
            landing.at[slot], load_sem.at[slot])

    steps = chi // CHUNK
    for step in range(SLOTS):
        load(step, step).start()

    @pl.when(first_site)
    def _():
        pltpu.make_async_copy(
            start_hbm, gathered.at[:, pl.ds(pl.multiple_of(me * cols, cols), cols)],
            start_sem).start()

    barrier = pltpu.get_barrier_semaphore()

    def greet(there, device):
        @pl.when(there)
        def _():
            pl.semaphore_signal(barrier, inc=1, device_id=device, device_id_type=MESH)

    around = ((has_up, {"bond": me + 2}), (has_down, {"bond": me - 2}),
              (chip >= 0, {"bond": pair}),
              (has_next, {"site": site + 1}), (site > 0, {"site": site - 1}))
    for there, device in around:
        greet(there, device)
    peers = sum(there.astype(jnp.int32) for there, _ in around)
    pl.semaphore_wait(barrier, peers)

    @pl.when(first_site)
    def _():
        pltpu.make_async_copy(
            start_hbm, gathered.at[:, pl.ds(pl.multiple_of(me * cols, cols), cols)],
            start_sem).wait()

    def spread(step, carry):
        slot = lax.rem(step, SLOTS)
        load(step, slot).wait()
        for t in range(cols // LANES):
            strip = slice(t * LANES, (t + 1) * LANES)
            wide[t] = landing[slot, :, :, strip].astype(jnp.float32).reshape(CHUNK * phys, LANES)
            for p in range(phys):
                mats[p, pl.ds(pl.multiple_of(step * CHUNK, CHUNK), CHUNK), strip] = (
                    wide[t, pl.ds(p, CHUNK, stride=phys), :].astype(jnp.bfloat16))

        @pl.when(step + SLOTS < steps)
        def _():
            load(step + SLOTS, slot).start()
        return carry

    for part in range(chips):
        @pl.when(first_site)
        def _():
            relay(0, part)
        lax.fori_loop(part * steps // chips, (part + 1) * steps // chips, spread, 0)

    @pl.when(jnp.logical_not(first_site))
    def _():
        for part in range(chips):
            relay(0, part)

    def batch(b, carry):
        for source in range(chips):
            arrived_pair(b, source)
        here = pl.ds(pl.multiple_of(b * rows, rows), rows)
        squares = jnp.zeros((rows, LANES), jnp.float32)
        for t in range(chi // LANES):
            x = gathered[here, t * LANES:(t + 1) * LANES].astype(jnp.float32)
            squares = squares + x * x
        norm = jnp.sqrt(jnp.sum(squares, axis=1, keepdims=True) / chi + 1e-06)
        log_ref[here, :] = jnp.log(norm)
        for p in range(phys):
            @pl.when(b + 1 < batches)
            def _():
                for part in range(p * chips // phys, (p + 1) * chips // phys):
                    relay(b + 1, part)
            prod = jnp.dot(gathered[here, :], mats[p], preferred_element_type=jnp.float32)
            prod = prod * scale_ref[p:p + 1, :] * weight_ref[here, p:p + 1]
            if p == 0:
                total[...] = prod
            elif p < phys - 1:
                total[...] += prod
            else:
                leave_ref[here, :] = ((total[...] + prod) / norm).astype(jnp.bfloat16)

        @pl.when(has_next)
        def _():
            site_copy(b).start()
        return carry

    lax.fori_loop(0, batches, batch, 0)

    def drain(b, carry):
        @pl.when(has_next)
        def _():
            site_copy(b).wait_send()
        for source in range(chips):
            pair_copy(b, source).wait_send()

            @pl.when(jnp.logical_and(has_up, source <= chip))
            def _():
                up_copy(b, source).wait_send()

            @pl.when(jnp.logical_and(has_down, source >= chip))
            def _():
                down_copy(b, source).wait_send()
        return carry

    lax.fori_loop(0, batches, drain, 0)


def local(start_rows, site_tensors, block_scales, displacement, outcomes):
    sites = lax.axis_size("site")
    bond = lax.axis_size("bond")
    _, chi, phys, cols = site_tensors.shape
    allrows = start_rows.shape[0]
    nblk = block_scales.shape[2]
    scales = jnp.repeat(block_scales[0], cols // nblk, axis=1)
    onehot = (outcomes[0][:, None] == jnp.arange(phys, dtype=jnp.int32)[None, :]).astype(jnp.float32)
    weight = jnp.sum(onehot[:, :, None] * displacement[0][None], axis=1)
    batches = allrows // min(ROWS, allrows)
    chips = bond // 2
    sems = pltpu.SemaphoreType.DMA
    leave, logs = pl.pallas_call(
        functools.partial(kernel, sites, bond),
        out_shape=(jax.ShapeDtypeStruct((allrows, cols), jnp.bfloat16),
                   jax.ShapeDtypeStruct((allrows, 1), jnp.float32)),
        in_specs=[pl.BlockSpec(memory_space=pl.ANY), pl.BlockSpec(memory_space=pl.ANY),
                  pl.BlockSpec(memory_space=pltpu.VMEM), pl.BlockSpec(memory_space=pltpu.VMEM)],
        out_specs=(pl.BlockSpec(memory_space=pltpu.VMEM), pl.BlockSpec(memory_space=pltpu.VMEM)),
        scratch_shapes=[
            pltpu.VMEM((phys, chi, cols), jnp.bfloat16),
            pltpu.VMEM((allrows, chi), jnp.bfloat16),
            pltpu.VMEM((SLOTS, CHUNK, phys, cols), jnp.bfloat16),
            pltpu.VMEM((cols // LANES, CHUNK * phys, LANES), jnp.float32),
            pltpu.VMEM((min(ROWS, allrows), cols), jnp.float32),
            sems(()), sems((SLOTS,)),
            sems((batches, chips)), sems((batches, chips)), sems((batches, chips)), sems((batches,)),
            sems((batches, chips)), sems((batches, chips)), sems((batches,)),
        ],
        compiler_params=pltpu.CompilerParams(
            collective_id=0, has_side_effects=True, vmem_limit_bytes=64000000),
    )(start_rows, site_tensors[0], scales, weight)
    return leave[None], logs[:, 0][None]


def solution(mesh):
    return jax.shard_map(
        local,
        mesh=mesh,
        in_specs=(
            P(None, "bond"),
            P("site", None, None, "bond"),
            P("site", None, "bond"),
            P("site", None, None),
            P("site", None),
        ),
        out_specs=(P("site", None, "bond"), P("site", None)),
        check_vma=False,
    )
```

time: 551 us -> 249 us (0.45)
  waiting for transfers between devices: 303 us -> 0 us
  Pallas kernels: 0 us -> 239 us
  matrix products: 115 us -> 0 us
  local copies, waits for them, and re-layouts: 66 us -> 4.61 us
  other arithmetic: 45.2 us -> 3.31 us
  between operations: 13.8 us -> 0.65 us
  starting transfers between devices: 6.45 us -> 0 us
    pallas_call x0 -> x1, Pallas kernels: none -> 239 us  [local(): pl.pallas_call(functools.partial(kernel, sites, bond), out_shape=(jax.Sha...]
    all_gather x5 -> x0, waiting for transfers between devices: 234 us -> none  [tick(): piece = lax.all_gather(rows_in, 'bond', axis=1, tiled=True)]
    dot_general x10 -> x0, matrix products: 115 us -> none  [the longest x5 113 us: tick(): total = jnp.dot(piece, a_mat, preferred_element_type=jnp.float32)]
    ppermute x5 -> x0, waiting for transfers between devices: 69 us -> none  [shifted(): lax.ppermute(value, axis, [(source, source + steps) for source in range(i...]
    while x15 -> x0, local copies, waits for them, and re-layouts: 40.9 us -> none
    reduce_sum x10 -> x1, other arithmetic: 23.9 us -> 0.78 us  [local(): weight = jnp.sum(onehot[:, :, None] * displacement[0][None], axis=1)]
    select_n x15 -> x0, other arithmetic: 21.3 us -> none  [the longest x5 10.4 us: tick(): jnp.where(valid, lax.dynamic_update_slice_in_dim(out_leave, leave, first,...]
    unnamed x9 -> x3, local copies, waits for them, and re-layouts: 23.3 us -> 2.94 us
  transfers between devices with their start and end apart: 10 -> 0, of which waited for: 10 -> 0; matrix products, arithmetic and copies ran while one was open for 0% -> 0% of each run, Pallas kernels for 0% -> 0%
where the time goes in v1:
time: 249 us; the launch traced here: 248 us
  Pallas kernels  239 us (96%)
  local copies, waits for them, and re-layouts  4.61 us (2%)
  other arithmetic  3.31 us (1%)
    pallas_call x1, Pallas kernels, local(): pl.pallas_call(functools.partial(kernel, sites, bond), out_shape=(jax.Sha...  239 us

profile of v1, /device:TPU:7, one launch (start us, length us, event | category | flops | bytes accessed | tf_op | source)
XLA Modules:
  0.0 247.8 jit_solution(16342565470073949389)
XLA Ops:
  0.6 0.0 copy-start
  0.6 0.7 copy-done
  1.3 0.7 broadcast_bitcast_fusion.scale_ref
  2.0 0.7 fusion
  2.7 0.8 multiply_reduce_fusion
  3.5 1.0 copy.7.weight_ref
  4.5 239.2 %shard_map.68 = (bf16[1024,512]{1,0:T(8,128)(2,1)}, f32[1024,1]{1,0:T(8,128)}) custom-call(bf16[1024,512]{1,0:T(8,128)(2,1)} %start_hbm.1, bf16[4096,8,512]{2,1,0:T(8,128)(2,1)} %bitcast.9, f32[8,512]{1,0:T(8,128)} %broadcast_bitcast_fusion.scale_ref, f32[1024,8]{1,0:T(8,128)} %copy.7.weight_ref), custom_call_target="tpu_custom_call" | custom-call | tf_op jit(solution)/shard_map/pallas_call | solution.py:239
  243.7 1.8 reduce
  245.5 2.3 copy.9
Async XLA Ops:
  0.6 0.7 copy-start
